TPU v7x, 256 devices: a whole 4x4x8 slice. The times are simulated.
256 devices in a mesh: prow: 8 (over z), pcol: 32 (over x, y, core).
Axes of the slice: x: 4, y: 4, z: 8, core: 2. Of those that a mesh axis runs over, the one named last changes fastest.
Arguments:
- inverse_tiles: float32 [8192, 8192], P('pcol', 'prow'), may hold values from -6 to 6
- factor: float32 [2, 8192, 512], P(None, ('pcol', 'prow')), may hold values from -0.09375 to 0.09375
- link_factor: float32 [1, 512, 512], replicated, may hold values from -0.25 to 0.25
- diag_inverse: float32 [2, 512, 512], replicated, may hold values from -3 to 3
- ancestors: int32 [2, 8], replicated, may hold values from 0 to 15, as said below
Outputs:
- offdiag: float32 [2, 8192, 512], P(None, ('pcol', 'prow'))
- diag: float32 [2, 512, 512], P(None, 'pcol')
- link_blocks: float32 [1, 512, 512], P(None, 'pcol')
Inputs may be any that keep to these rules, and one draw needn't show every extreme that they name: `ancestors`: row k lists 8 distinct stored block rows; every row lists block 15, and row 0 lists block 0.
All inputs are finite; a program needn't handle non-finite values.
Results may differ from a plain program's by a relative error of at most 0.0001.
Values sent between devices are 32-bit elements; how exact they have to be, the bound alone decides.
A program may use at most 64 MiB of HBM per device.

v0:
```python
import jax
import jax.numpy as jnp
from jax import lax
from jax.sharding import PartitionSpec as P


def broadcast(value, axis, source):
    kept = jnp.where(lax.axis_index(axis) == source, value, 0).astype(value.dtype)
    return lax.psum(kept, axis)


def product(left_part, right_part):
    return jnp.dot(
        left_part, right_part, precision=lax.Precision.HIGHEST, preferred_element_type=jnp.float32
    )


def gather_columns(row_factor, ratio, prow_index, concat_dim):
    pieces = []
    for member in range(ratio):
        pieces.append(broadcast(row_factor, "pcol", prow_index * ratio + member))
    return jnp.concatenate(pieces, axis=concat_dim)


def body(inverse_tiles, factor, link_factor, diag_inverse, ancestors):
    row_count, col_count = inverse_tiles.shape
    nsuper, unit_rows, columns = factor.shape
    prow_count = lax.axis_size("prow")
    pcol_count = lax.axis_size("pcol")
    ratio = col_count // row_count
    prow_index = lax.axis_index("prow")
    pcol_index = lax.axis_index("pcol")
    first_row = (pcol_index * prow_count + prow_index) * unit_rows
    block_ids = (first_row + lax.iota(jnp.int32, unit_rows)) // columns
    selected = jnp.any(block_ids[None, :, None] == ancestors[:, None, :], axis=2).astype(
        jnp.float32
    )
    unit_factor = factor * selected[:, :, None]
    slice_rows = columns // pcol_count
    slice_start = pcol_index * slice_rows
    offdiag_list = []
    diag_list = []
    link_list = []
    prior_offdiag = None
    prior_diag = None
    for number in range(nsuper):
        row_factor = lax.all_gather(unit_factor[number], "prow", axis=0, tiled=True)
        col_factor = gather_columns(row_factor, ratio, prow_index, 0)

        def partial_term(begin_row, row_total, col_factor=col_factor):
            return product(inverse_tiles, col_factor)

        summed = lax.psum_scatter(
            partial_term(jnp.int32(0), lax.axis_size("prow") * unit_rows),
            "prow",
            scatter_dimension=0,
            tiled=True,
        )
        local_factor = unit_factor[number]
        gram_part = product(local_factor.T, summed)
        keep_rows = selected[number][:, None]
        if number == 0:
            gram_sum = lax.psum(gram_part, ("prow", "pcol"))
            result = -(keep_rows * summed)
            diag_block = diag_inverse[0] + gram_sum
        else:
            link_block = link_factor[number - 1]
            cross_part = product(prior_offdiag.T, local_factor)
            gram_sum, cross_sum = lax.psum((gram_part, cross_part), ("prow", "pcol"))
            result = -(keep_rows * (summed + product(prior_offdiag, link_block)))
            link_out = -(cross_sum + product(prior_diag, link_block))
            diag_block = (
                diag_inverse[number]
                + gram_sum
                + product(cross_sum.T, link_block)
                - product(link_block.T, link_out)
            )
            link_list.append(lax.dynamic_slice_in_dim(link_out, slice_start, slice_rows, 0))
        offdiag_list.append(result)
        diag_list.append(lax.dynamic_slice_in_dim(diag_block, slice_start, slice_rows, 0))
        prior_offdiag = result
        prior_diag = diag_block
    return (jnp.stack(offdiag_list), jnp.stack(diag_list), jnp.stack(link_list))


def solution(mesh):
    in_specs = (P("pcol", "prow"), P(None, ("pcol", "prow"), None), P(), P(), P())
    out_specs = (P(None, ("pcol", "prow"), None), P(None, "pcol", None), P(None, "pcol", None))
    return jax.shard_map(body, mesh=mesh, in_specs=in_specs, out_specs=out_specs, check_vma=False)
```

profile of v0, /device:TPU:2, one launch (start us, length us, event | category | flops | bytes accessed | tf_op | source)
XLA Modules:
  0.0 558.0 jit_solution(3136330771844192)
XLA Ops:
  7.2 0.0 copy-start
  7.2 0.0 all-reduce.7.cloned.1.call-start
  7.3 0.8 compare_reduce_fusion
  8.1 1.0 broadcast_multiply_fusion
  9.1 29.1 %all-gather = f32[1,256,512]{2,1,0:T(8,128)S(1)} all-gather(f32[1,32,512]{2,1,0:T(8,128)S(1)} %get-tuple-element.25), channel_id=2, replica_groups=mesh['prow'=8,'pcol'=32] {'prow'}, dimensions={1}, use_global_device_ids=true | all-gather | bytes 589824 | tf_op jit(solution)/shard_map/all_gather | solution.py:47
  38.2 25.6 %all-gather.1 = f32[1,256,512]{2,1,0:T(8,128)S(1)} all-gather(f32[1,32,512]{2,1,0:T(8,128)S(1)} %get-tuple-element.26), channel_id=3, replica_groups=mesh['prow'=8,'pcol'=32] {'prow'}, dimensions={1}, use_global_device_ids=true | all-gather | bytes 589824 | tf_op jit(solution)/shard_map/all_gather | solution.py:47
  63.8 1.4 select_bitcast_fusion.7
  65.3 1.4 select_bitcast_fusion.3
  66.7 0.0 copy-start.4
  66.7 0.0 all-reduce.7.cloned.1.call-update
  66.7 0.0 reduce-scatter.7.cloned.1.call-start
  66.8 121.3 %all-reduce.7.cloned.1.call-done = (f32[256,512]{1,0:T(8,128)}, f32[256,512]{1,0:T(8,128)}, f32[256,512]{1,0:T(8,128)}, f32[256,512]{1,0:T(8,128)}, f32[256,512]...) async-done(((f32[256,512]{1,0:T(8,128)}, f32[256,512]{1,0:T(8,128)}, f32[256,512]{1,0:T(8,128)}, f32[256,512]{1,0:T(8,128)}, ...) | async-done | bytes 4194320 | tf_op jit(solution)/shard_map/psum | solution.py:9
  188.1 0.0 copy-done.4
  188.1 0.0 copy-start.5
  188.1 5.0 fusion.20
  193.1 1.0 copy.14
  194.1 0.0 reduce-scatter.7.cloned.1.call-update
  194.1 0.0 reduce-scatter.9.cloned.1.call-start
  194.2 0.0 copy-done.5
  194.2 4.8 fusion.17
  199.0 1.0 copy.16
  200.0 0.0 reduce-scatter.9.cloned.1.call-update
  200.0 0.2 all-reduce.5.cloned.1.call-start
  200.3 31.7 %reduce-scatter.7.cloned.1.call-done = f32[32,512]{1,0:T(8,128)} async-done(((f32[256,512]{1,0:T(8,128)}), f32[32,512]{1,0:T(8,128)}) %reduce-scatter.7.cloned.1.call-update) | async-done | bytes 65552
  231.9 1.0 copy.15
  232.9 2.8 fusion.38
  235.7 2.0 fusion.31
  237.7 0.0 copy-start.2
  237.7 33.2 %reduce-scatter.9.cloned.1.call-done = f32[32,512]{1,0:T(8,128)} async-done(((f32[256,512]{1,0:T(8,128)}), f32[32,512]{1,0:T(8,128)}) %reduce-scatter.9.cloned.1.call-update) | async-done | bytes 65552
  270.9 2.9 fusion.35
  273.8 0.0 all-reduce.5.cloned.1.call-update
  273.8 0.0 copy-start.3
  273.8 0.0 copy-done.2
  273.8 1.1 slice_bitcast_fusion
  274.9 0.7 fusion.32
  275.6 1.0 copy.13
  276.6 0.0 copy-done
  276.6 0.0 copy-done.3
  276.6 0.7 fusion.25
  277.3 0.7 pad_maximum_fusion
  278.0 264.3 %all-reduce.5.cloned.1.call-done = (f32[512,512]{1,0:T(8,128)}, f32[512,512]{1,0:T(8,128)}, f32[512,512]{1,0:T(8,128)}) async-done(((f32[512,512]{1,0:T(8,128)}, f32[512,512]{1,0:T(8,128)}, f32[512,512]{1,0:T(8,128)}), (f32[512,512]{1,0:T(8,128)}, f32[512,512]{1,0:T(8,128)}, f32[512,512]{1,0:T(8,128)})) %all-reduce.5.cloned.1.call-update) | async-done | bytes 3145744 | tf_op jit(solution)/shard_map/psum | solution.py:69
  542.3 1.5 bitcast_add_fusion
  543.8 0.0 copy-done.1
  543.8 1.9 fusion.28
  545.7 1.9 fusion.16
  547.5 1.9 convolution_bitcast_fusion
  549.5 1.4 fusion.40
  550.9 0.6 pad_maximum_fusion.1
  (6 shorter events, 0.0 us)
Async XLA Ops:
  7.2 269.5 %copy-start = (f32[1,512,512]{2,1,0:T(8,128)S(1)}, f32[1,512,512]{2,1,0:T(8,128)}, u32[]{:S(2)}) copy-start(f32[1,512,512]{2,1,0:T(8,128)} %param.7) | copy-start | bytes 3145732
  7.2 180.9 %all-reduce.7.cloned.1.call-start = ((), (), s32[]{:S(2)}) async-start(), calls=%async_computation.5 | async-start | bytes 8388608 | tf_op jit(solution)/shard_map/psum | solution.py:9
  66.7 121.4 %copy-start.4 = (f32[256,1024]{1,0:T(8,128)S(1)}, f32[256,1024]{1,0:T(8,128)}, u32[]{:S(2)}) copy-start(f32[256,1024]{1,0:T(8,128)} %param.5) | copy-start | bytes 3145732
  66.7 165.2 %reduce-scatter.7.cloned.1.call-start = ((), (), s32[]{:S(2)}) async-start(), calls=%async_computation.2 | async-start | bytes 589824
  188.1 6.1 %copy-start.5 = (f32[256,512]{1,0:T(8,128)S(1)}, f32[256,512]{1,0:T(8,128)}, u32[]{:S(2)}) copy-start(f32[256,512]{1,0:T(8,128)} %get-tuple-element.9) | copy-start | bytes 1572868
  194.1 76.8 %reduce-scatter.9.cloned.1.call-start = ((), (), s32[]{:S(2)}) async-start(), calls=%async_computation.3 | async-start | bytes 589824
  200.0 342.3 %all-reduce.5.cloned.1.call-start = ((), (), s32[]{:S(2)}) async-start(), calls=%async_computation.4 | async-start | bytes 6291456 | tf_op jit(solution)/shard_map/psum | solution.py:69
  237.7 36.1 %copy-start.2 = (f32[2,512,512]{2,1,0:T(8,128)S(1)}, f32[2,512,512]{2,1,0:T(8,128)}, u32[]{:S(2)}) copy-start(f32[2,512,512]{2,1,0:T(8,128)} %param.8) | copy-start | bytes 6291460
  273.8 2.8 copy-start.3
  542.3 1.5 copy-start.1
Sparse Core Ops, SparseCore 0:
  66.8 121.1 all-reduce.6
  194.2 37.6 reduce-scatter.6
  234.5 36.4 reduce-scatter.8
  276.5 265.7 all-reduce.4
where the time goes:
time: 558 us
  waiting for transfers between devices  450 us (81%)
  blocking collectives  54.7 us (10%)
  matrix products  23.8 us (4%)
  between operations  13.9 us (2%)
  other arithmetic  9.63 us (2%)
    psum x1, waiting for transfers between devices, body(): gram_sum, cross_sum = lax.psum((gram_part, cross_part), ('prow', 'pcol'))  264 us
    psum x1, waiting for transfers between devices, broadcast(): return lax.psum(kept, axis)  121 us
    unnamed x6, waiting for transfers between devices  64.9 us
    all_gather x2, blocking collectives, body(): row_factor = lax.all_gather(unit_factor[number], 'prow', axis=0, tiled=True)  54.7 us
    dot_general x9, matrix products, product(): jnp.dot(left_part, right_part, precision=lax.Precision.HIGHEST, preferred...  23.8 us
  transfers between devices with their start and end apart: 4, of which 4 were waited for; matrix products, arithmetic and copies ran while one was open for 3% of the time, Pallas kernels for 0%

commit v1 on v0

--- a/solution.py
+++ b/solution.py
@@ -66,7 +66,7 @@
         else:
             link_block = link_factor[number - 1]
             cross_part = product(prior_offdiag.T, local_factor)
-            gram_sum, cross_sum = lax.psum((gram_part, cross_part), ("prow", "pcol"))
+            gram_sum, cross_sum = lax.psum(lax.psum((gram_part, cross_part), "pcol"), "prow")
             result = -(keep_rows * (summed + product(prior_offdiag, link_block)))
             link_out = -(cross_sum + product(prior_diag, link_block))
             diag_block = (

time: 558 us -> 754 us (1.35)
  waiting for transfers between devices: 450 us -> 645 us
    psum x1 -> x3, waiting for transfers between devices: 264 us -> 456 us  [the longest x1 262 us: body(): gram_sum = lax.psum(gram_part, ('prow', 'pcol'))]
    unnamed x6 -> x8, waiting for transfers between devices: 64.9 us -> 68 us
  transfers between devices with their start and end apart: 4 -> 6, of which waited for: 4 -> 6; matrix products, arithmetic and copies ran while one was open for 3% -> 2% of each run, Pallas kernels for 0% -> 0%
where the time goes in v1:
time: 754 us
  waiting for transfers between devices  645 us (86%)
  blocking collectives  54.7 us (7%)
  matrix products  25.2 us (3%)
  between operations  14.3 us (2%)
  other arithmetic  9.2 us (1%)
    psum x1, waiting for transfers between devices, body(): gram_sum = lax.psum(gram_part, ('prow', 'pcol'))  262 us
    psum x1, waiting for transfers between devices, broadcast(): return lax.psum(kept, axis)  121 us
    psum x1, waiting for transfers between devices, body(): lax.psum((gram_part, cross_part), 'pcol')  113 us
    psum x1, waiting for transfers between devices, body(): lax.psum(lax.psum((gram_part, cross_part), 'pcol'), 'prow')  81.6 us
    unnamed x8, waiting for transfers between devices  68 us
    all_gather x2, blocking collectives, body(): row_factor = lax.all_gather(unit_factor[number], 'prow', axis=0, tiled=True)  54.7 us
    dot_general x9, matrix products, product(): jnp.dot(left_part, right_part, precision=lax.Precision.HIGHEST, preferred...  25.2 us
  transfers between devices with their start and end apart: 6, of which 6 were waited for; matrix products, arithmetic and copies ran while one was open for 2% of the time, Pallas kernels for 0%

profile of v1, /device:TPU:2, one launch (start us, length us, event | category | flops | bytes accessed | tf_op | source)
XLA Modules:
  0.0 753.5 jit_solution(9574245205419443425)
XLA Ops:
  7.2 0.0 copy-start
  7.2 0.0 all-reduce.12.cloned.1.call-start
  7.3 0.8 compare_reduce_fusion
  8.1 1.0 broadcast_multiply_fusion
  9.1 29.1 %all-gather = f32[1,256,512]{2,1,0:T(8,128)S(1)} all-gather(f32[1,32,512]{2,1,0:T(8,128)S(1)} %get-tuple-element.26), channel_id=2, replica_groups=mesh['prow'=8,'pcol'=32] {'prow'}, dimensions={1}, use_global_device_ids=true | all-gather | bytes 589824 | tf_op jit(solution)/shard_map/all_gather | solution.py:47
  38.2 25.6 %all-gather.1 = f32[1,256,512]{2,1,0:T(8,128)S(1)} all-gather(f32[1,32,512]{2,1,0:T(8,128)S(1)} %get-tuple-element.27), channel_id=3, replica_groups=mesh['prow'=8,'pcol'=32] {'prow'}, dimensions={1}, use_global_device_ids=true | all-gather | bytes 589824 | tf_op jit(solution)/shard_map/all_gather | solution.py:47
  63.8 1.4 select_bitcast_fusion.7
  65.3 1.4 select_bitcast_fusion.3
  66.7 0.0 all-reduce.12.cloned.1.call-update
  66.7 0.0 reduce-scatter.7.cloned.1.call-start
  66.8 121.3 %all-reduce.12.cloned.1.call-done = (f32[256,512]{1,0:T(8,128)}, f32[256,512]{1,0:T(8,128)}, f32[256,512]{1,0:T(8,128)}, f32[256,512]{1,0:T(8,128)}, f32[256,512...) async-done(((f32[256,512]{1,0:T(8,128)}, f32[256,512]{1,0:T(8,128)}, f32[256,512]{1,0:T(8,128)}, f32[256,512]{1,0:T(8,128)}, ...) | async-done | bytes 4194320 | tf_op jit(solution)/shard_map/psum | solution.py:9
  188.1 0.0 copy-done.4
  188.1 5.0 fusion.20
  193.1 1.0 copy.14
  194.1 0.0 reduce-scatter.7.cloned.1.call-update
  194.1 0.0 reduce-scatter.9.cloned.1.call-start
  194.2 4.8 fusion.17
  199.0 1.0 copy.16
  200.0 0.0 reduce-scatter.9.cloned.1.call-update
  200.0 0.0 all-reduce.10.cloned.1.call-start
  200.1 31.8 %reduce-scatter.7.cloned.1.call-done = f32[32,512]{1,0:T(8,128)} async-done(((f32[256,512]{1,0:T(8,128)}), f32[32,512]{1,0:T(8,128)}) %reduce-scatter.7.cloned.1.call-update) | async-done | bytes 65552
  231.9 1.0 copy.15
  232.9 1.9 fusion.31
  234.8 36.1 %reduce-scatter.9.cloned.1.call-done = f32[32,512]{1,0:T(8,128)} async-done(((f32[256,512]{1,0:T(8,128)}), f32[32,512]{1,0:T(8,128)}) %reduce-scatter.9.cloned.1.call-update) | async-done | bytes 65552
  270.9 2.9 fusion.35
  273.8 0.0 all-reduce.10.cloned.1.call-update
  273.8 0.0 copy-start.2
  273.8 0.0 all-reduce.8.cloned.1.call-start
  273.9 3.0 fusion.38
  276.9 0.0 all-reduce.8.cloned.1.call-update
  276.9 0.2 all-reduce.14.cloned.1.call-start
  277.1 112.6 %all-reduce.10.cloned.1.call-done = (f32[512,512]{1,0:T(8,128)}, f32[512,512]{1,0:T(8,128)}) async-done(((f32[512,512]{1,0:T(8,128)}, f32[512,512]{1,0:T(8,128)}), (f32[512,512]{1,0:T(8,128)}, f32[512,512]{1,0:T(8,128)})) %all-reduce.10.cloned.1.call-update) | async-done | bytes 2097168 | tf_op jit(solution)/shard_map/psum | solution.py:69
  389.7 0.0 all-reduce.14.cloned.1.call-update
  389.7 1.1 slice_bitcast_fusion
  390.8 0.1 copy.13
  390.9 0.0 copy-done
  390.9 0.0 copy-done.3
  390.9 0.7 fusion.25
  391.7 0.7 pad_maximum_fusion
  392.3 262.0 %all-reduce.8.cloned.1.call-done = f32[512,512]{1,0:T(8,128)} async-done(((f32[512,512]{1,0:T(8,128)}), f32[512,512]{1,0:T(8,128)}) %all-reduce.8.cloned.1.call-update) | async-done | bytes 1048592 | tf_op jit(solution)/shard_map/psum | solution.py:63
  654.3 1.7 bitcast_add_fusion
  656.1 81.6 %all-reduce.14.cloned.1.call-done = (f32[512,512]{1,0:T(8,128)}, f32[512,512]{1,0:T(8,128)}) async-done(((f32[512,512]{1,0:T(8,128)}, f32[512,512]{1,0:T(8,128)}), (f32[512,512]{1,0:T(8,128)}, f32[512,512]{1,0:T(8,128)})) %all-reduce.14.cloned.1.call-update) | async-done | bytes 2097168 | tf_op jit(solution)/shard_map/psum | solution.py:69
  737.7 3.2 fusion.16
  740.9 0.0 copy-done.1
  740.9 1.8 fusion.28
  742.8 1.9 convolution_bitcast_fusion
  744.6 1.4 fusion.40
  746.1 0.6 pad_maximum_fusion.1
  (12 shorter events, 0.1 us)
Async XLA Ops:
  7.2 383.8 %copy-start = (f32[1,512,512]{2,1,0:T(8,128)S(1)}, f32[1,512,512]{2,1,0:T(8,128)}, u32[]{:S(2)}) copy-start(f32[1,512,512]{2,1,0:T(8,128)} %param.7) | copy-start | bytes 3145732
  7.2 180.9 %all-reduce.12.cloned.1.call-start = ((), (), s32[]{:S(2)}) async-start(), calls=%async_computation.6 | async-start | bytes 8388608 | tf_op jit(solution)/shard_map/psum | solution.py:9
  66.7 121.4 %copy-start.4 = (f32[256,1024]{1,0:T(8,128)S(1)}, f32[256,1024]{1,0:T(8,128)}, u32[]{:S(2)}) copy-start(f32[256,1024]{1,0:T(8,128)} %param.5) | copy-start | bytes 3145732
  66.7 165.2 %reduce-scatter.7.cloned.1.call-start = ((), (), s32[]{:S(2)}) async-start(), calls=%async_computation.3 | async-start | bytes 589824
  188.1 6.1 copy-start.5
  194.1 76.8 %reduce-scatter.9.cloned.1.call-start = ((), (), s32[]{:S(2)}) async-start(), calls=%async_computation.4 | async-start | bytes 589824
  200.0 189.7 %all-reduce.10.cloned.1.call-start = ((), (), s32[]{:S(2)}) async-start(), calls=%async_computation.5 | async-start | bytes 4194304 | tf_op jit(solution)/shard_map/psum | solution.py:69
  273.8 115.9 %copy-start.2 = (f32[2,512,512]{2,1,0:T(8,128)S(1)}, f32[2,512,512]{2,1,0:T(8,128)}, u32[]{:S(2)}) copy-start(f32[2,512,512]{2,1,0:T(8,128)} %param.8) | copy-start | bytes 6291460
  273.8 380.5 %all-reduce.8.cloned.1.call-start = ((), (), s32[]{:S(2)}) async-start(), calls=%async_computation.2 | async-start | bytes 2097152 | tf_op jit(solution)/shard_map/psum | solution.py:63
  276.9 460.8 %all-reduce.14.cloned.1.call-start = ((), (), s32[]{:S(2)}) async-start(), calls=%async_computation.7 | async-start | bytes 4194304 | tf_op jit(solution)/shard_map/psum | solution.py:69
  389.7 1.2 copy-start.3
  737.7 3.2 copy-start.1
Sparse Core Ops, SparseCore 0:
  66.9 121.1 all-reduce.11
  194.3 37.6 reduce-scatter.6
  234.4 36.4 reduce-scatter.8
  274.1 115.5 all-reduce.9
  395.0 259.2 all-reduce.7
  656.6 81.1 all-reduce.13
